TPU v7x, 256 devices: a whole 4x4x8 slice. The times are simulated.
256 devices in a mesh: layer: 32 (over y, z), xs: 8 (over x, core).
Axes of the slice: x: 4, y: 4, z: 8, core: 2. Of those that a mesh axis runs over, the one named last changes fastest.
Arguments:
- probes: float32 [64, 32, 16, 640], P('layer', None, 'xs'), may hold values from -6 to 6
- potential: float32 [64, 16, 640], P('layer', 'xs'), may hold values from -1 to 1
- projector: bfloat16 [64, 512, 1280], P('layer', 'xs'), may hold values from -0.15625 to 0.15625
- intersection_ids: int32 [64, 512], P('layer', 'xs'), may hold values from 0 to 255
- strength: float32 [64, 256], P('layer'), may hold values from -2 to 2
- decay_rates: float32 [64, 32], P('layer'), may hold values from 0.3 to 1
- contour_nodes: float32 [4], replicated, may hold values from -1 to 3
- node_weights: float32 [4], replicated, may hold values from 0.5 to 1.5
Outputs:
- moments: float32 [2, 64, 32, 16, 640], P(None, 'layer', None, 'xs')
All inputs are finite; a program needn't handle non-finite values.
Results may differ from a plain program's by a relative error of at most 0.00059.
Values sent between devices are 32-bit elements; how exact they have to be, the bound alone decides.
A program may use at most 64 MiB of HBM per device.

v0:
```python
import jax
import jax.numpy as jnp
from jax import lax
from jax.sharding import PartitionSpec as P

NPROJ = 256
FAR = -1.0 / 12.0
NEAR = 4.0 / 3.0
CENTER = -2.5


def carried_in(part, axis, combine, identity, reverse):
    count = lax.axis_size(axis)
    place = lax.axis_index(axis)
    ahead = count - 1 - place if reverse else place
    gathered = jax.tree.map(lambda a: lax.all_gather(a, axis), part)
    state = jax.tree.map(lambda a, e: jnp.zeros_like(a) + jnp.asarray(e, a.dtype), part, identity)

    def one(lap, state):
        source = count - 1 - lap if reverse else lap
        return combine(
            state, jax.tree.map(lambda a: lax.dynamic_index_in_dim(a, source, 0, False), gathered)
        )

    return lax.fori_loop(0, ahead, one, state)


def with_halo(cells, sides, width):
    for axis, dim in sides:
        count = lax.axis_size(axis)
        ends = count - 1
        head = lax.slice_in_dim(cells, 0, width, axis=dim)
        tail = lax.slice_in_dim(cells, cells.shape[dim] - width, cells.shape[dim], axis=dim)
        cells = jnp.concatenate(
            [
                lax.ppermute(tail, axis, [(i, (i + 1) % count) for i in range(ends)]),
                cells,
                lax.ppermute(head, axis, [((i + 1) % count, i) for i in range(ends)]),
            ],
            axis=dim,
        )
    return cells


def second_along(padded, axis, count):

    def piece(offset):
        return lax.slice_in_dim(padded, 2 + offset, 2 + offset + count, axis=axis)

    return FAR * (piece(-2) + piece(2)) + NEAR * (piece(-1) + piece(1)) + CENTER * piece(0)


def combine(earlier, later):
    return (earlier[0] * later[0], later[0][:, None, None] * earlier[1] + later[1])


def scan_sweeps(forcing, decay_rates):
    count = forcing.shape[1]
    zero = jnp.zeros_like(forcing[:, 0])
    through = jnp.prod(decay_rates, axis=0)
    state = zero
    ahead_list = []
    for index in range(count):
        rate = decay_rates[index][:, None, None]
        state = rate * state + (1.0 - rate) * forcing[:, index]
        ahead_list.append(state)
    ahead_zero = jnp.stack(ahead_list, axis=1)
    entering = carried_in(
        (through, ahead_zero[:, -1]), "layer", combine, (jnp.ones_like(through), zero), False
    )[1]
    lower_prod = jnp.cumprod(decay_rates, axis=0)
    ahead = ahead_zero + lower_prod[None, :, :, None, None] * entering[:, None]
    state = zero
    back_list = []
    for index in reversed(range(count)):
        rate = decay_rates[index][:, None, None]
        state = rate * state + (1.0 - rate) * ahead[:, index]
        back_list.append(state)
    back_zero = jnp.stack(back_list[::-1], axis=1)
    from_above = carried_in(
        (through, back_zero[:, 0]), "layer", combine, (jnp.ones_like(through), zero), True
    )[1]
    upper_prod = jnp.cumprod(decay_rates[::-1], axis=0)[::-1]
    return back_zero + upper_prod[None, :, :, None, None] * from_above[:, None]


def run_sweeps(forcing, decay_rates):
    return scan_sweeps(forcing, decay_rates)


def shards(
    probes,
    potential,
    projector,
    intersection_ids,
    strength,
    decay_rates,
    contour_nodes,
    node_weights,
):
    layers, columns, rows, depth = probes.shape
    padded = with_halo(probes, (("layer", 0), ("xs", 2)), 2)
    across = jnp.pad(probes, ((0, 0), (0, 0), (0, 0), (2, 2)))
    laplace = second_along(padded[:, :, 2:-2, :], 0, layers)
    laplace = laplace + second_along(padded[2:-2], 2, rows)
    laplace = laplace + second_along(across, 3, depth)
    rounded = probes.astype(jnp.bfloat16).reshape(layers, columns, rows * depth)
    slot_coef = jnp.einsum("lsp,lcp->lsc", projector, rounded, preferred_element_type=jnp.float32)
    onehot = (intersection_ids[:, :, None] == jnp.arange(NPROJ, dtype=jnp.int32)).astype(
        jnp.float32
    )
    partial_coef = jnp.einsum("lsq,lsc->lqc", onehot, slot_coef, precision=lax.Precision.HIGHEST)
    coef = lax.psum(partial_coef, "xs")
    scaled = (strength[:, :, None] * coef).astype(jnp.bfloat16)
    slot_back = jnp.einsum(
        "lsq,lqc->lsc", onehot.astype(jnp.bfloat16), scaled, preferred_element_type=jnp.float32
    ).astype(jnp.bfloat16)
    projected = jnp.einsum(
        "lsp,lsc->lcp", projector, slot_back, preferred_element_type=jnp.float32
    ).reshape(layers, columns, rows, depth)
    hamil = -0.5 * laplace + potential[:, None] * probes + projected
    forcing = hamil[None] - contour_nodes[:, None, None, None, None] * probes[None]
    swept = run_sweeps(forcing, decay_rates)
    first = jnp.sum(node_weights[:, None, None, None, None] * swept, axis=0)
    second = jnp.sum((node_weights * contour_nodes)[:, None, None, None, None] * swept, axis=0)
    return jnp.stack([first, second])


def solution(mesh):
    in_specs = (
        P("layer", None, "xs", None),
        P("layer", "xs", None),
        P("layer", "xs", None),
        P("layer", "xs"),
        P("layer", None),
        P("layer", None),
        P(),
        P(),
    )
    out_specs = P(None, "layer", None, "xs", None)
    return jax.shard_map(shards, mesh=mesh, in_specs=in_specs, out_specs=out_specs, check_vma=False)
```

profile of v0, /device:TPU:1, one launch (start us, length us, event | category | flops | bytes accessed | tf_op | source)
XLA Modules:
  0.0 558.4 jit_solution(769351655144849599)
XLA Ops:
  6.5 4.5 collective-permute-start
  11.1 1.3 collective-permute-start.1
  12.4 5.4 collective-permute-done
  17.8 2.0 constant_dynamic-update-slice_fusion.1
  19.8 2.0 collective-permute-done.1
  21.9 3.6 collective-permute-start.3
  25.5 3.0 collective-permute-start.2
  31.5 62.9 %all-reduce.4.cloned.1.call-done = f32[2,256,32]{1,2,0:T(8,128)} async-done(((f32[2,256,32]{1,2,0:T(8,128)}), f32[2,256,32]{1,2,0:T(8,128)}) %all-reduce.4.cloned.1.call-update) | async-done | bytes 65552 | tf_op jit(solution)/shard_map/psum | solution.py:113
  94.4 1.9 fusion.2
  96.3 1.9 reshape.101
  98.2 3.2 add_add_fusion
  104.4 61.3 %all-reduce.1 = f32[1024]{0:T(1024)S(1)} all-reduce(f32[1024]{0:T(1024)S(1)} %dynamic-update-slice), channel_id=2, replica_groups=mesh['layer'=32,'xs'=8] {'layer'}, use_global_device_ids=true, to_apply=%add.1 | all-reduce | flops 1024 | bytes 8192
  166.0 99.1 %all-gather.4.cloned.1.call-done = f32[32,4,32,2,640]{4,2,3,1,0:T(8,128)} async-done(((f32[1,4,32,2,640]{4,2,3,1,0:T(8,128)}), f32[32,4,32,2,640]{4,2,3,1,0:T(8,128)}) %all-gather.4.cloned.1.call-update) | async-done | bytes 20971536 | tf_op jit(solution)/shard_map/all_gather | solution.py:16
  267.0 219.5 %all-gather.6.cloned.1.call-done = f32[32,4,32,2,640]{4,2,3,1,0:T(8,128)} async-done(((f32[1,4,32,2,640]{4,2,3,1,0:T(8,128)}), f32[32,4,32,2,640]{4,2,3,1,0:T(8,128)}) %all-gather.6.cloned.1.call-update) | async-done | bytes 20971536 | tf_op jit(solution)/shard_map/all_gather | solution.py:16
  486.7 63.4 %while.27 = (s32[]{:T(128)}, f32[4,32,2,640]{3,2,1,0:T(2,128)S(1)}, s32[]{:T(128)}, f32[32,32]{1,0:T(8,128)S(1)}, f32[32,4,32,2,640]{4,2,3,1,0:T(8,128)}, /*index=5*/s32[]{:T(128)}, s32[]{:T(128)}, s32[]{:T(128)}, s32[]{:T(128)}) while((s32[]{:T(128)}, f32[4,32,2,640]{3,2,1,0:T(2,128)S(1)}, s32[]{:T(128)}, f32[32,32]{1,0:T(8,128)S(1)}, ...), condition=%wide.region_7.8_spmd, body=%wide.region_6.7_spmd.sunk | while | flops 327686 | bytes 3277339 | solution.py:25
  486.7 1.1 constant_dynamic-slice_fusion.5
  488.7 1.1 constant_dynamic-slice_fusion.5
  490.8 1.1 constant_dynamic-slice_fusion.5
  492.8 1.1 constant_dynamic-slice_fusion.5
  494.9 1.1 constant_dynamic-slice_fusion.5
  496.9 1.1 constant_dynamic-slice_fusion.5
  499.0 1.1 constant_dynamic-slice_fusion.5
  501.0 1.1 constant_dynamic-slice_fusion.5
  503.1 1.1 constant_dynamic-slice_fusion.5
  505.1 1.1 constant_dynamic-slice_fusion.5
  507.2 1.1 constant_dynamic-slice_fusion.5
  509.2 1.1 constant_dynamic-slice_fusion.5
  511.2 1.1 constant_dynamic-slice_fusion.5
  521.5 1.1 constant_dynamic-slice_fusion.5
  525.6 1.1 constant_dynamic-slice_fusion.5
  529.7 1.1 constant_dynamic-slice_fusion.5
  550.6 1.3 copy.21
  (137 shorter events, 52.1 us)
Async XLA Ops:
  6.5 23.0 %copy-start = (bf16[2,64,1280]{2,1,0:T(8,128)(2,1)S(1)}, bf16[2,64,1280]{2,1,0:T(8,128)(2,1)}, u32[]{:S(2)}) copy-start(bf16[2,64,1280]{2,1,0:T(8,128)(2,1)} %param.14) | copy-start | bytes 983044
  6.5 22.0 %copy-start.3 = (f32[2,32]{1,0:T(2,128)S(1)}, f32[2,32]{1,0:T(2,128)}, u32[]{:S(2)}) copy-start(f32[2,32]{1,0:T(2,128)} %param.17) | copy-start | bytes 772
  6.5 87.8 %all-reduce.4.cloned.1.call-start = ((), (), s32[]{:S(2)}) async-start(), calls=%async_computation | async-start | bytes 131072 | tf_op jit(solution)/shard_map/psum | solution.py:113
  6.5 11.2 %collective-permute-start = (f32[2,32,2,640]{3,2,1,0:T(2,128)}, f32[2,32,2,640]{3,2,1,0:T(2,128)S(1)}, u32[]{:S(2)}, u32[]{:S(2)}) collective-permute-start(f32[2,32,2,640]{3,2,1,0:T(2,128)} %param.12), channel_id=1, source_target_pairs={{0,8},{8,16},{16,24},{24,32},{32,40},{40,48},{48,56},{56,64},{64,7... | collective-permute-start | bytes 983048 | tf_op jit(solution)/shard_map/ppermute | solution.py:36
  11.1 10.7 %collective-permute-start.1 = (f32[2,32,2,640]{3,2,1,0:T(2,128)}, f32[2,32,2,640]{3,2,1,0:T(2,128)S(1)}, u32[]{:S(2)}, u32[]{:S(2)}) collective-permute-start(f32[2,32,2,640]{3,2,1,0:T(2,128)} %param.12), channel_id=1, source_target_pairs={{8,0},{16,8},{24,16},{32,24},{40,32},{48,40},{56,48},{64,56},{72,6... | collective-permute-start | bytes 983048 | tf_op jit(solution)/shard_map/ppermute | solution.py:38
  17.8 12.0 %copy-start.5 = (s32[2,64]{1,0:T(2,128)S(1)}, s32[2,64]{1,0:T(2,128)}, u32[]{:S(2)}) copy-start(s32[2,64]{1,0:T(2,128)} %param.15) | copy-start | bytes 1540
  17.8 13.0 %copy-start.1 = (f32[2,32,2,640]{3,2,1,0:T(2,128)S(1)}, f32[2,32,2,640]{3,2,1,0:T(2,128)}, u32[]{:S(2)}) copy-start(f32[2,32,2,640]{3,2,1,0:T(2,128)} %param.12) | copy-start | bytes 983044
  19.8 74.6 %copy-start.6 = (f32[2,256]{1,0:T(2,128)S(1)}, f32[2,256]{1,0:T(2,128)}, u32[]{:S(2)}) copy-start(f32[2,256]{1,0:T(2,128)} %param.16) | copy-start | bytes 6148
  21.9 76.3 %collective-permute-start.3 = (f32[6,32,2,640]{3,2,1,0:T(2,128)S(1)}, f32[6,32,2,640]{3,2,1,0:T(2,128)S(1)}, u32[]{:S(2)}, u32[]{:S(2)}) collective-permute-start(f32[6,32,2,640]{3,2,1,0:T(2,128)S(1)} %constant_dynamic-update-slice_fusion), channel_id=1, source_target_pairs={{1,0},{2,1},{3,2},{4,3},{5,4},{6,5},{7,6},{9,8},{10,9},{11,10},{12... | collective-permute-start | bytes 2949128 | tf_op jit(solution)/shard_map/ppermute | solution.py:38
  25.5 72.8 %collective-permute-start.2 = (f32[6,32,2,640]{3,2,1,0:T(2,128)S(1)}, f32[6,32,2,640]{3,2,1,0:T(2,128)}, u32[]{:S(2)}, u32[]{:S(2)}) collective-permute-start(f32[6,32,2,640]{3,2,1,0:T(2,128)S(1)} %constant_dynamic-update-slice_fusion), channel_id=1, source_target_pairs={{0,1},{1,2},{2,3},{3,4},{4,5},{5,6},{6,7},{8,9},{9,10},{10,11},{11... | collective-permute-start | bytes 2949128 | tf_op jit(solution)/shard_map/ppermute | solution.py:36
  29.5 68.7 %copy-start.4 = (f32[2,2,640]{2,1,0:T(2,128)S(1)}, f32[2,2,640]{2,1,0:T(2,128)}, u32[]{:S(2)}) copy-start(f32[2,2,640]{2,1,0:T(2,128)} %param.13) | copy-start | bytes 30724
  30.7 234.5 %all-gather.4.cloned.1.call-start = ((), (), s32[]{:S(2)}) async-start(), calls=%async_computation.1 | async-start | bytes 21626880 | tf_op jit(solution)/shard_map/all_gather | solution.py:16
  98.2 3.2 copy-start.2
  98.2 3.2 copy-start.7
  101.7 1.2 copy-start.9
  102.7 383.8 %all-gather.6.cloned.1.call-start = ((), (), s32[]{:S(2)}) async-start(), calls=%async_computation.2 | async-start | bytes 21626880 | tf_op jit(solution)/shard_map/all_gather | solution.py:16
  265.6 1.2 copy-start.8
Sparse Core Ops, SparseCore 0:
  30.8 63.5 all-reduce.3
  102.8 162.2 all-gather.3
  268.1 218.3 all-gather.5
where the time goes:
time: 560 us; the launch traced here: 558 us
  waiting for transfers between devices  389 us (69%)
  blocking collectives  61.3 us (11%)
  local copies, waits for them, and re-layouts  42.2 us (8%)
  other arithmetic  35.2 us (6%)
  between operations  14.1 us (3%)
  starting transfers between devices  12.5 us (2%)
    all_gather x2, waiting for transfers between devices, carried_in(): gathered = jax.tree.map(lambda a: lax.all_gather(a, axis), part)  319 us
    psum x1, waiting for transfers between devices, shards(): coef = lax.psum(partial_coef, 'xs')  62.9 us
    unnamed x1, blocking collectives  61.3 us
    dynamic_slice x31, local copies, waits for them, and re-layouts, one(): lax.dynamic_index_in_dim(a, source, 0, False)  35.2 us
    add x31, other arithmetic, combine(): later[0][:, None, None] * earlier[1] + later[1]  26.7 us
  transfers between devices with their start and end apart: 7, of which 5 were waited for; matrix products, arithmetic and copies ran while one was open for 2% of the time, Pallas kernels for 0%

commit v1 on v0

--- a/solution.py
+++ b/solution.py
@@ -110,7 +110,7 @@
         jnp.float32
     )
     partial_coef = jnp.einsum("lsq,lsc->lqc", onehot, slot_coef, precision=lax.Precision.HIGHEST)
-    coef = lax.psum(partial_coef, "xs")
+    coef = jnp.sum(lax.all_gather(partial_coef, "xs"), axis=0)
     scaled = (strength[:, :, None] * coef).astype(jnp.bfloat16)
     slot_back = jnp.einsum(
         "lsq,lqc->lsc", onehot.astype(jnp.bfloat16), scaled, preferred_element_type=jnp.float32

time: 560 us -> 515 us (0.920)
  waiting for transfers between devices: 389 us -> 324 us
  blocking collectives: 61.3 us -> 78.8 us
    psum x1 -> x0, waiting for transfers between devices: 62.9 us -> none  [shards(): coef = lax.psum(partial_coef, 'xs')]
    all_gather x0 -> x1, blocking collectives: none -> 16.3 us  [shards(): coef = jnp.sum(lax.all_gather(partial_coef, 'xs'), axis=0)]
  transfers between devices with their start and end apart: 7 -> 6, of which waited for: 5 -> 4; matrix products, arithmetic and copies ran while one was open for 2% -> 2% of each run, Pallas kernels for 0% -> 0%
where the time goes in v1:
time: 515 us; the launch traced here: 513 us
  waiting for transfers between devices  324 us (63%)
  blocking collectives  78.8 us (15%)
  local copies, waits for them, and re-layouts  43.4 us (8%)
  other arithmetic  36.4 us (7%)
  between operations  14.2 us (3%)
  starting transfers between devices  12.5 us (2%)
    all_gather x2, waiting for transfers between devices, carried_in(): gathered = jax.tree.map(lambda a: lax.all_gather(a, axis), part)  318 us
    unnamed x1, blocking collectives  62.5 us
    dynamic_slice x31, local copies, waits for them, and re-layouts, one(): lax.dynamic_index_in_dim(a, source, 0, False)  35.2 us
    add x31, other arithmetic, combine(): later[0][:, None, None] * earlier[1] + later[1]  26.7 us
    all_gather x1, blocking collectives, shards(): coef = jnp.sum(lax.all_gather(partial_coef, 'xs'), axis=0)  16.3 us
  transfers between devices with their start and end apart: 6, of which 4 were waited for; matrix products, arithmetic and copies ran while one was open for 2% of the time, Pallas kernels for 0%

profile of v1, /device:TPU:1, one launch (start us, length us, event | category | flops | bytes accessed | tf_op | source)
XLA Modules:
  0.0 513.0 jit_solution(17840394112578787337)
XLA Ops:
  6.5 4.5 collective-permute-start
  11.1 1.3 collective-permute-start.1
  12.4 1.2 broadcast_multiply_fusion.1
  13.6 4.1 collective-permute-done
  17.8 2.0 constant_dynamic-update-slice_fusion.1
  19.8 2.0 collective-permute-done.1
  21.9 3.6 collective-permute-start.3
  25.5 3.0 collective-permute-start.2
  31.3 16.3 %all-gather = f32[16,256,32]{1,2,0:T(8,128)S(1)} all-gather(f32[2,256,32]{1,2,0:T(8,128)S(1)} %fusion.21), channel_id=2, replica_groups=mesh['layer'=32,'xs'=8] {'xs'}, dimensions={0}, use_global_device_ids=true | all-gather | bytes 589824 | tf_op jit(solution)/shard_map/all_gather | solution.py:113
  47.7 1.8 fusion.2
  49.5 1.9 reshape.101
  51.4 3.2 add_add_fusion
  57.8 62.5 %all-reduce.1 = f32[1024]{0:T(1024)S(1)} all-reduce(f32[1024]{0:T(1024)S(1)} %dynamic-update-slice), channel_id=3, replica_groups=mesh['layer'=32,'xs'=8] {'layer'}, use_global_device_ids=true, to_apply=%add.1 | all-reduce | flops 1024 | bytes 8192
  120.6 98.5 %all-gather.5.cloned.1.call-done = f32[32,4,32,2,640]{4,2,3,1,0:T(8,128)} async-done(((f32[1,4,32,2,640]{4,2,3,1,0:T(8,128)}), f32[32,4,32,2,640]{4,2,3,1,0:T(8,128)}) %all-gather.5.cloned.1.call-update) | async-done | bytes 20971536 | tf_op jit(solution)/shard_map/all_gather | solution.py:16
  221.2 219.5 %all-gather.7.cloned.1.call-done = f32[32,4,32,2,640]{4,2,3,1,0:T(8,128)} async-done(((f32[1,4,32,2,640]{4,2,3,1,0:T(8,128)}), f32[32,4,32,2,640]{4,2,3,1,0:T(8,128)}) %all-gather.7.cloned.1.call-update) | async-done | bytes 20971536 | tf_op jit(solution)/shard_map/all_gather | solution.py:16
  440.9 63.4 %while.27 = (s32[]{:T(128)}, f32[4,32,2,640]{3,2,1,0:T(2,128)S(1)}, s32[]{:T(128)}, f32[32,32]{1,0:T(8,128)S(1)}, f32[32,4,32,2,640]{4,2,3,1,0:T(8,128)}, /*index=5*/s32[]{:T(128)}, s32[]{:T(128)}, s32[]{:T(128)}, s32[]{:T(128)}) while((s32[]{:T(128)}, f32[4,32,2,640]{3,2,1,0:T(2,128)S(1)}, s32[]{:T(128)}, f32[32,32]{1,0:T(8,128)S(1)}, ...), condition=%wide.region_7.8_spmd, body=%wide.region_6.7_spmd.sunk | while | flops 327686 | bytes 3277339 | solution.py:25
  440.9 1.1 constant_dynamic-slice_fusion.5
  443.0 1.1 constant_dynamic-slice_fusion.5
  445.0 1.1 constant_dynamic-slice_fusion.5
  447.1 1.1 constant_dynamic-slice_fusion.5
  449.1 1.1 constant_dynamic-slice_fusion.5
  451.2 1.1 constant_dynamic-slice_fusion.5
  453.2 1.1 constant_dynamic-slice_fusion.5
  455.3 1.1 constant_dynamic-slice_fusion.5
  457.3 1.1 constant_dynamic-slice_fusion.5
  459.4 1.1 constant_dynamic-slice_fusion.5
  461.4 1.1 constant_dynamic-slice_fusion.5
  463.4 1.1 constant_dynamic-slice_fusion.5
  492.1 1.1 constant_dynamic-slice_fusion.5
  496.2 1.1 constant_dynamic-slice_fusion.5
  500.3 1.1 constant_dynamic-slice_fusion.5
  504.8 1.3 copy.21
  (142 shorter events, 53.8 us)
Async XLA Ops:
  6.5 24.3 %copy-start = (bf16[2,64,1280]{2,1,0:T(8,128)(2,1)S(1)}, bf16[2,64,1280]{2,1,0:T(8,128)(2,1)}, u32[]{:S(2)}) copy-start(bf16[2,64,1280]{2,1,0:T(8,128)(2,1)} %param.14) | copy-start | bytes 983044
  6.5 22.6 %copy-start.1 = (f32[2,32,2,640]{3,2,1,0:T(2,128)S(1)}, f32[2,32,2,640]{3,2,1,0:T(2,128)}, u32[]{:S(2)}) copy-start(f32[2,32,2,640]{3,2,1,0:T(2,128)} %param.12) | copy-start | bytes 983044
  6.5 22.0 %copy-start.5 = (f32[2,32]{1,0:T(2,128)S(1)}, f32[2,32]{1,0:T(2,128)}, u32[]{:S(2)}) copy-start(f32[2,32]{1,0:T(2,128)} %param.17) | copy-start | bytes 772
  6.5 212.5 %all-gather.5.cloned.1.call-start = ((), (), s32[]{:S(2)}) async-start(), calls=%async_computation | async-start | bytes 21626880 | tf_op jit(solution)/shard_map/all_gather | solution.py:16
  6.5 11.2 %collective-permute-start = (f32[2,32,2,640]{3,2,1,0:T(2,128)}, f32[2,32,2,640]{3,2,1,0:T(2,128)S(1)}, u32[]{:S(2)}, u32[]{:S(2)}) collective-permute-start(f32[2,32,2,640]{3,2,1,0:T(2,128)} %param.12), channel_id=1, source_target_pairs={{0,8},{8,16},{16,24},{24,32},{32,40},{40,48},{48,56},{56,64},{64,7... | collective-permute-start | bytes 983048 | tf_op jit(solution)/shard_map/ppermute | solution.py:36
  11.1 10.7 %collective-permute-start.1 = (f32[2,32,2,640]{3,2,1,0:T(2,128)}, f32[2,32,2,640]{3,2,1,0:T(2,128)S(1)}, u32[]{:S(2)}, u32[]{:S(2)}) collective-permute-start(f32[2,32,2,640]{3,2,1,0:T(2,128)} %param.12), channel_id=1, source_target_pairs={{8,0},{16,8},{24,16},{32,24},{40,32},{48,40},{56,48},{64,56},{72,6... | collective-permute-start | bytes 983048 | tf_op jit(solution)/shard_map/ppermute | solution.py:38
  17.8 13.3 %copy-start.9 = (s32[2,64]{1,0:T(2,128)S(1)}, s32[2,64]{1,0:T(2,128)}, u32[]{:S(2)}) copy-start(s32[2,64]{1,0:T(2,128)} %param.15) | copy-start | bytes 1540
  21.8 9.3 %copy-start.2 = (f32[2,32,2,640]{3,2,1,0:T(2,128)}, f32[2,32,2,640]{3,2,1,0:T(2,128)S(1)}, u32[]{:S(2)}) copy-start(f32[2,32,2,640]{3,2,1,0:T(2,128)S(1)} %collective-permute-done.1) | copy-start | bytes 983044
  21.9 29.5 %collective-permute-start.3 = (f32[6,32,2,640]{3,2,1,0:T(2,128)S(1)}, f32[6,32,2,640]{3,2,1,0:T(2,128)S(1)}, u32[]{:S(2)}, u32[]{:S(2)}) collective-permute-start(f32[6,32,2,640]{3,2,1,0:T(2,128)S(1)} %constant_dynamic-update-slice_fusion), channel_id=1, source_target_pairs={{1,0},{2,1},{3,2},{4,3},{5,4},{6,5},{7,6},{9,8},{10,9},{11,10},{12... | collective-permute-start | bytes 2949128 | tf_op jit(solution)/shard_map/ppermute | solution.py:38
  25.5 25.9 %collective-permute-start.2 = (f32[6,32,2,640]{3,2,1,0:T(2,128)S(1)}, f32[6,32,2,640]{3,2,1,0:T(2,128)}, u32[]{:S(2)}, u32[]{:S(2)}) collective-permute-start(f32[6,32,2,640]{3,2,1,0:T(2,128)S(1)} %constant_dynamic-update-slice_fusion), channel_id=1, source_target_pairs={{0,1},{1,2},{2,3},{3,4},{4,5},{5,6},{6,7},{8,9},{9,10},{10,11},{11... | collective-permute-start | bytes 2949128 | tf_op jit(solution)/shard_map/ppermute | solution.py:36
  47.6 3.8 copy-start.3
  51.4 3.3 copy-start.4
  51.4 3.3 copy-start.10
  54.6 0.6 copy-start.7
  54.6 0.7 copy-start.8
  55.3 1.2 copy-start.12
  56.3 384.4 %all-gather.7.cloned.1.call-start = ((), (), s32[]{:S(2)}) async-start(), calls=%async_computation.1 | async-start | bytes 21626880 | tf_op jit(solution)/shard_map/all_gather | solution.py:16
  219.3 0.6 copy-start.6
  219.9 1.1 copy-start.11
Sparse Core Ops, SparseCore 0:
  56.4 162.5 all-gather.4
  221.6 219.0 all-gather.6
